TPU v7x, 512 devices: a whole 4x8x8 slice. The times are simulated.
512 devices in a mesh: chrom: 8 (over x, y_hi), samp: 64 (over z, y_lo, core).
Axes of the slice: x: 4, y: 8 (y_hi: 2, y_lo: 4; y = y_hi * 4 + y_lo), z: 8, core: 2. Of those that a mesh axis runs over, the one named last changes fastest.
Arguments:
- genotypes: int32 [24576, 24576], P('samp', 'chrom'), may hold values from 0 to 2, as said below
- frequency: float32 [24576], P('chrom'), may hold values from 0.05 to 0.5, as said below
- widths: int32 [8], replicated, may hold values from 1 to 6144, 24576 in all
- ridge_term: float32 [1], replicated, may hold values from 0.5 to 1.5
- direction: float32 [24576, 64], P('samp'), may hold values from -6 to 6
Outputs:
- loco_out: float32 [8, 24576, 64], P('chrom', 'samp')
Inputs may be any that keep to these rules, and one draw needn't show every extreme that they name: Each variant's allele frequency is a whole number of thousandths. `genotypes`: each dosage, apart from samples 0 and 1 at variant 0 (set to 2 and 0), is the sum of two independent draws that are 1 with the variant's allele frequency and 0 otherwise. The 8 widths sum to 24576.
All inputs are finite; a program needn't handle non-finite values.
Results may differ from a plain program's by a relative error of at most 0.004.
Values may be sent and summed in bfloat16 or wider, within the bound.
A program may use at most 64 MiB of HBM per device.

v0:
```python
import jax
import jax.numpy as jnp
from jax import lax
from jax.sharding import PartitionSpec as P


def cut_along(x, dim, count):
    before, after = (x.shape[:dim], x.shape[dim + 1 :])
    return jnp.moveaxis(x.reshape(*before, count, -1, *after), dim, 0)


def summed_on_arrival(x, axis, dim):
    blocks = cut_along(x, dim, lax.axis_size(axis))
    arrived = lax.all_to_all(blocks, axis, split_axis=0, concat_axis=0, tiled=True)
    return arrived.sum(axis=0)


def from_everyone(x, axis):
    copies = jnp.broadcast_to(x, (lax.axis_size(axis), *x.shape))
    return lax.all_to_all(copies, axis, split_axis=0, concat_axis=0, tiled=True)


def joined_along(blocks, dim):
    blocks = jnp.moveaxis(blocks, 0, dim)
    dims = blocks.shape
    return blocks.reshape(*dims[:dim], dims[dim] * dims[dim + 1], *dims[dim + 2 :])


def gather_directly(x, axis, dim):
    blocks = from_everyone(x, axis)
    return joined_along(blocks, dim)


def taken_together(x, axis):
    return from_everyone(x, axis).sum(axis=0)


def on_device(genotypes, frequency, widths, ridge_term, direction):
    local_vars = genotypes.shape[1]
    sample_rows = genotypes.shape[0]
    sections_all = widths.shape[0]
    rhs_count = direction.shape[1]
    doubled = 2.0 * frequency
    standard = (
        (genotypes.astype(jnp.float32) - doubled) * lax.rsqrt(doubled * (1.0 - frequency))
    ).astype(jnp.bfloat16)
    vector = direction.astype(jnp.bfloat16)
    first_var = lax.axis_index("chrom") * local_vars
    section_ends = jnp.cumsum(widths)
    var_index = first_var + jnp.arange(local_vars, dtype=jnp.int32)
    section = jnp.sum((var_index[:, None] >= section_ends[None, :]).astype(jnp.int32), axis=1)
    onehot = (section[:, None] == jnp.arange(sections_all, dtype=jnp.int32)[None, :]).astype(
        jnp.bfloat16
    )
    contract = (((0,), (0,)), ((), ()))
    columns = standard
    crossed = summed_on_arrival(
        lax.dot_general(columns, vector, contract, preferred_element_type=jnp.float32), "samp", 0
    )
    shared = crossed.astype(jnp.bfloat16)
    portion = gather_directly(shared, "samp", 0)
    length = portion.shape[0]
    columns = standard
    spread = (portion[:, None, :] * onehot[:, :, None]).reshape(length, sections_all * rhs_count)
    partial_value = jnp.dot(columns, spread, preferred_element_type=jnp.float32)
    per_device = sections_all // lax.axis_size("chrom")
    first_section = lax.axis_index("chrom") * per_device
    by_section = partial_value.reshape(sample_rows, sections_all, rhs_count)
    own_sums = summed_on_arrival(by_section, "chrom", 1)
    all_total = taken_together(jnp.sum(by_section, axis=1), "chrom")
    variant_total = local_vars * lax.axis_size("chrom")
    own_widths = lax.dynamic_slice_in_dim(widths, first_section, per_device, 0)
    divisor = (variant_total - own_widths).astype(jnp.float32)
    result = (
        ridge_term[0] * direction[:, None, :]
        + (all_total[:, None, :] - own_sums) / divisor[None, :, None]
    )
    return jnp.transpose(result, (1, 0, 2))


def solution(mesh):
    return jax.shard_map(
        on_device,
        mesh=mesh,
        in_specs=(P("samp", "chrom"), P("chrom"), P(), P(), P("samp", None)),
        out_specs=P("chrom", "samp", None),
        check_vma=False,
    )
```

profile of v0, /device:TPU:1, one launch (start us, length us, event | category | flops | bytes accessed | tf_op | source)
XLA Modules:
  0.0 131.6 jit_solution(10675806944754782705)
XLA Ops:
  0.0 0.7 broadcast_multiply_fusion.1
  0.7 0.0 copy-start.1
  0.7 3.5 %fusion.1 = f32[3072,64]{1,0:T(8,128)S(1)} fusion(s32[384,3072]{1,0:T(8,128)} %param.5, f32[3072]{0:T(1024)S(1)} %get-tuple-element.6, f32[3072]{0:T(1024)S(1)} %get-tuple-element.5, f32[384,64]{0,1:T(8,128)} %param.9), kind=kOutput, calls=%fused_computation.3 | convolution fusion | flops 155738112 | bytes 5627904 | tf_op jit(solution)/shard_map/reshape | solution.py:9
  4.2 1.9 %reshape.78 = f32[64,1,3072]{2,1,0:T(1,128)} reshape(f32[64,48,64]{2,1,0:T(8,128)S(1)} %bitcast.17) | data formatting | bytes 1572864
  6.1 15.4 %all-to-all-start = ((f32[64,1,3072]{2,1,0:T(1,128)}), f32[64,1,3072]{2,1,0:T(1,128)S(1)}, u32[]{:S(2)}, u32[]{:S(2)}) async-start(f32[64,1,3072]{2,1,0:T(1,128)} %reshape.78), calls=%async_computation | async-start | bytes 1572864 | tf_op jit(solution)/shard_map/all_to_all | solution.py:14
  21.5 0.0 copy-done.1
  21.5 0.2 reduce-window.8
  21.7 23.5 %all-to-all-done = f32[64,1,3072]{2,1,0:T(1,128)S(1)} async-done(((f32[64,1,3072]{2,1,0:T(1,128)}), f32[64,1,3072]{2,1,0:T(1,128)S(1)}, u32[]{:S(2)}, u32[]{:S(2)}) %all-to-all-start) | async-done | bytes 786464 | tf_op jit(solution)/shard_map/all_to_all | solution.py:14
  45.1 0.5 broadcast.26
  45.6 2.5 %reduce.1 = f32[64,3072]{1,0:T(8,128)S(1)} reduce(f32[64,1,3072]{2,1,0:T(1,128)S(1)} %all-to-all-done, f32[]{:T(128)} %broadcast.26), dimensions={1}, to_apply=%all_to_all.12.reduce_sub_computation | reduce | bytes 1572868 | tf_op jit(solution)/shard_map/all_to_all | solution.py:14
  48.1 0.4 reshape.79
  48.6 0.1 reduce_sum.45
  48.7 0.1 broadcast_in_dim.4
  48.8 1.2 reshape.80
  50.0 5.3 %all-to-all-start.1 = ((bf16[64,2,1536]{2,1,0:T(2,128)(2,1)}), bf16[64,2,1536]{2,1,0:T(2,128)(2,1)S(1)}, u32[]{:S(2)}, u32[]{:S(2)}) async-start(bf16[64,2,1536]{2,1,0:T(2,128)(2,1)} %reshape.80), calls=%async_computation.1 | async-start | bytes 786432 | tf_op jit(solution)/shard_map/all_to_all | solution.py:20
  55.4 0.1 convert_reduce_fusion
  55.5 16.0 %all-to-all-done.1 = bf16[64,2,1536]{2,1,0:T(2,128)(2,1)S(1)} async-done(((bf16[64,2,1536]{2,1,0:T(2,128)(2,1)}), bf16[64,2,1536]{2,1,0:T(2,128)(2,1)S(1)}, u32[]{:S(2)}, u32[]{:S(2)}) %all-to-all-start.1) | async-done | bytes 393248 | tf_op jit(solution)/shard_map/all_to_all | solution.py:20
  71.5 0.5 reshape.81
  71.9 0.3 copy.22
  72.2 0.3 broadcast_multiply_fusion
  72.5 5.1 %fusion = f32[384,512]{0,1:T(8,128)} fusion(bf16[3072,512]{0,1:T(8,128)(2,1)S(1)} %bitcast.18, s32[384,3072]{1,0:T(8,128)} %param.5, f32[3072]{0:T(1024)S(1)} %get-tuple-element.6, f32[3072]{0:T(1024)S(1)} %get-tuple-element.5), kind=kOutput, calls=%fused_computation.2 | convolution fusion | flops 1212678144 | bytes 8675328 | tf_op jit(solution)/shard_map/dot_general | solution.py:65
  77.6 0.0 copy-start
  77.6 1.2 reduce_sum.47
  78.8 0.1 broadcast_in_dim.5
  78.9 28.3 %all_to_all.20 = f32[8,384,64]{1,2,0:T(8,128)S(1)} all-to-all(f32[8,384,64]{1,2,0:T(8,128)S(1)} %broadcast_in_dim.5), channel_id=1, replica_groups=mesh['chrom'=8,'samp'=64] {'chrom'}, dimensions={0} | all-to-all | bytes 1572864 | tf_op jit(solution)/shard_map/all_to_all | solution.py:20
  107.2 3.5 %all-to-all-start.3 = ((f32[8,384,1,64]{1,3,2,0:T(8,128)}), f32[8,384,1,64]{1,3,2,0:T(8,128)S(1)}, u32[]{:S(2)}, u32[]{:S(2)}) async-start(f32[8,384,1,64]{1,3,2,0:T(8,128)} %bitcast.9), calls=%async_computation.3 | async-start | bytes 1572864 | tf_op jit(solution)/shard_map/all_to_all | solution.py:14
  110.7 0.6 dynamic_slice.3
  112.7 18.3 %all-to-all-done.3 = f32[8,384,1,64]{1,3,2,0:T(8,128)S(1)} async-done(((f32[8,384,1,64]{1,3,2,0:T(8,128)}), f32[8,384,1,64]{1,3,2,0:T(8,128)S(1)}, u32[]{:S(2)}, u32[]{:S(2)}) %all-to-all-start.3) | async-done | bytes 786464 | tf_op jit(solution)/shard_map/all_to_all | solution.py:14
  131.0 0.0 copy-done
  131.0 0.7 add_bitcast_fusion
  (4 shorter events, 0.1 us)
Async XLA Ops:
  0.7 20.8 %copy-start.1 = (s32[8]{0:T(128)S(1)}, s32[8]{0:T(128)}, u32[]{:S(2)}) copy-start(s32[8]{0:T(128)} %param.7) | copy-start | bytes 100
  6.1 39.1 %all-to-all-start = ((f32[64,1,3072]{2,1,0:T(1,128)}), f32[64,1,3072]{2,1,0:T(1,128)S(1)}, u32[]{:S(2)}, u32[]{:S(2)}) async-start(f32[64,1,3072]{2,1,0:T(1,128)} %reshape.78), calls=%async_computation | async-start | bytes 1572864 | tf_op jit(solution)/shard_map/all_to_all | solution.py:14
  50.0 21.4 %all-to-all-start.1 = ((bf16[64,2,1536]{2,1,0:T(2,128)(2,1)}), bf16[64,2,1536]{2,1,0:T(2,128)(2,1)S(1)}, u32[]{:S(2)}, u32[]{:S(2)}) async-start(bf16[64,2,1536]{2,1,0:T(2,128)(2,1)} %reshape.80), calls=%async_computation.1 | async-start | bytes 786432 | tf_op jit(solution)/shard_map/all_to_all | solution.py:20
  77.6 53.4 %copy-start = (f32[384,64]{0,1:T(8,128)S(1)}, f32[384,64]{0,1:T(8,128)}, u32[]{:S(2)}) copy-start(f32[384,64]{0,1:T(8,128)} %param.9) | copy-start | bytes 294916
  107.2 23.8 %all-to-all-start.3 = ((f32[8,384,1,64]{1,3,2,0:T(8,128)}), f32[8,384,1,64]{1,3,2,0:T(8,128)S(1)}, u32[]{:S(2)}, u32[]{:S(2)}) async-start(f32[8,384,1,64]{1,3,2,0:T(8,128)} %bitcast.9), calls=%async_computation.3 | async-start | bytes 1572864 | tf_op jit(solution)/shard_map/all_to_all | solution.py:14
where the time goes:
time: 134 us; the launch traced here: 132 us
  waiting for transfers between devices  57.7 us (43%)
  blocking collectives  28.3 us (21%)
  starting transfers between devices  24.3 us (18%)
  matrix products  8.56 us (6%)
  other arithmetic  5.89 us (4%)
  local copies, waits for them, and re-layouts  5.5 us (4%)
  between operations  1.44 us (1%)
    all_to_all x2, waiting for transfers between devices, summed_on_arrival(): lax.all_to_all(blocks, axis, split_axis=0, concat_axis=0, tiled=True)  41.7 us
    all_to_all x1, blocking collectives, from_everyone(): return lax.all_to_all(copies, axis, split_axis=0, concat_axis=0, tiled=True)  28.3 us
    all_to_all x2, starting transfers between devices, summed_on_arrival(): lax.all_to_all(blocks, axis, split_axis=0, concat_axis=0, tiled=True)  18.9 us
    all_to_all x1, waiting for transfers between devices, from_everyone(): return lax.all_to_all(copies, axis, split_axis=0, concat_axis=0, tiled=True)  16 us
    all_to_all x1, starting transfers between devices, from_everyone(): return lax.all_to_all(copies, axis, split_axis=0, concat_axis=0, tiled=True)  5.32 us
    dot_general x1, matrix products, on_device(): partial_value = jnp.dot(columns, spread, preferred_element_type=jnp.float32)  5.09 us
    unnamed x8, local copies, waits for them, and re-layouts  3.98 us
    reshape x1, matrix products, cut_along(): return jnp.moveaxis(x.reshape(*before, count, -1, *after), dim, 0)  3.48 us
  transfers between devices with their start and end apart: 3, of which 3 were waited for; matrix products, arithmetic and copies ran while one was open for 1% of the time, Pallas kernels for 0%

commit v1 on v0

v1 whole, which is shorter than its diff:
```python
import jax
import jax.numpy as jnp
from jax import lax
from jax.experimental import pallas as pl
from jax.experimental.pallas import tpu as pltpu
from jax.sharding import PartitionSpec as P

MESH = pl.DeviceIdType.MESH
NZ, NY, NCORE = 8, 4, 2
NX, NH = 4, 2
BF16, F32 = jnp.bfloat16, jnp.float32


def far_first(i):
    half = NZ // 2
    return lax.rem(jnp.where(lax.rem(i, 2) == 1, half + (i + 1) // 2, half - i // 2), NZ)


def near_first(i):
    return lax.rem(jnp.where(lax.rem(i, 2) == 1, (i + 1) // 2, NZ - i // 2), NZ)


def kernel(
    gen_hbm, freq_ref, widths_ref, ridge_ref, dir_ref, out_ref,
    gbuf, std, own, psend, precv, rsend, rrecv, shared, acc, xsend, xrecv, ysend, yrecv, bounds,
    gsem, psend_sem, precv_sem, rsend_sem, rrecv_sem, asend_sem, arecv_sem, fsend_sem, frecv_sem,
    xsend_sem, xrecv_sem, ysend_sem, yrecv_sem,
):
    rhs, rows = dir_ref.shape
    group = gbuf.shape[2]
    variants = NX * NH * NZ * group
    ci, si = lax.axis_index("chrom"), lax.axis_index("samp")
    z, y, core = si // (NY * NCORE), lax.rem(si // NCORE, NY), lax.rem(si, NCORE)
    x, yh = ci // NH, lax.rem(ci, NH)

    def samp_dev(off, dq):
        return (ci, (lax.rem(z + off, NZ) * NY + lax.rem(y + dq, NY)) * NCORE + core)

    partner = (ci, si + 1 - 2 * core)

    def chrom_dev(dx, dh):
        return (lax.rem(x + dx, NX) * NH + lax.rem(yh + dh, NH), si)

    def lane_group(off):
        return lax.rem(z + off, NZ)

    def gcopy(i):
        lanes = pl.ds(pl.multiple_of(lane_group(far_first(i)) * group, 128), group)
        return pltpu.make_async_copy(gen_hbm.at[:, lanes], gbuf.at[i], gsem.at[i])

    def start_gcopy(i, _):
        gcopy(i).start()
        return 0

    lax.fori_loop(0, NZ, start_gcopy, 0)

    barrier = pltpu.get_barrier_semaphore()
    peers = 0
    for off in (4, 5, 3, 6, 2, 7, 1, 0):
        for dq in range(NY):
            if off or dq:
                pl.semaphore_signal(barrier, inc=1, device_id=samp_dev(off, dq), device_id_type=MESH)
                peers += 1
    for dx, dh in ((0, 1), (2, 0), (1, 0), (3, 0)):
        pl.semaphore_signal(barrier, inc=1, device_id=chrom_dev(dx, dh), device_id_type=MESH)
        peers += 1
    pl.semaphore_signal(barrier, inc=1, device_id=partner, device_id_type=MESH)
    peers += 1

    total = jnp.int32(0)
    for c in range(NX * NH):
        bounds[0, c] = total
        total = total + widths_ref[c]
        bounds[1, c] = total

    vector = dir_ref[...].astype(BF16)

    def first_products(i, _):
        gcopy(i).wait()
        lg = lane_group(far_first(i))
        freq = freq_ref[:, pl.ds(pl.multiple_of(lg * group, 128), group)]
        doubled = 2.0 * freq
        scale = lax.rsqrt(doubled * (1.0 - freq))
        block = ((gbuf[i].astype(F32) - doubled) * scale).astype(BF16)
        std[lg] = block
        own[i] = jnp.dot(vector, block, preferred_element_type=F32)
        return 0

    lax.fori_loop(0, NZ, first_products, 0)

    pl.semaphore_wait(barrier, peers)

    half = rhs // NCORE

    def pair_copy(i):
        return pltpu.make_async_remote_copy(
            src_ref=psend.at[i], dst_ref=precv.at[i],
            send_sem=psend_sem.at[i], recv_sem=precv_sem.at[i],
            device_id=partner, device_id_type=MESH,
        )

    def pair_start(i, _):
        theirs = pl.multiple_of((1 - core) * half, half)
        psend[i] = own[i, pl.ds(theirs, half), :].astype(BF16)
        pair_copy(i).start()
        return 0

    lax.fori_loop(0, NZ, pair_start, 0)

    def scatter_copy(i, off, dq):
        return pltpu.make_async_remote_copy(
            src_ref=rsend.at[i, lax.rem(y + dq, NY)], dst_ref=rrecv.at[off, dq],
            send_sem=rsend_sem, recv_sem=rrecv_sem.at[off],
            device_id=samp_dev(off, dq), device_id_type=MESH,
        )

    def pair_sum(i):
        pair_copy(i).wait()
        mine = pl.multiple_of(core * half, half)
        value = own[i, pl.ds(mine, half), :] + precv[i].astype(F32)
        rsend[i] = value.astype(BF16).reshape(NY, half // NY, group)

    def scatter(i, _):
        pair_sum(i)
        off = far_first(i)
        for dq in (2, 3, 1, 0):
            scatter_copy(i, off, dq).start()
        return 0

    lax.fori_loop(0, NZ - 1, scatter, 0)
    pair_sum(NZ - 1)
    for dq in range(1, NY):
        scatter_copy(NZ - 1, 0, dq).start()

    block = rsend[NZ - 1, y].astype(F32)
    for off in (0, 1, 7, 2, 6, 3, 5, 4):
        part = rrecv.at[off, pl.ds(1, NY - 1)] if off == 0 else rrecv.at[off]
        pltpu.make_async_copy(part, part, rrecv_sem.at[off]).wait()
        for dq in range(NY):
            if off or dq:
                block = block + rrecv[off, dq].astype(F32)
    shared[z, core, y] = block.astype(BF16)

    def gather_copy(off, dq):
        return pltpu.make_async_remote_copy(
            src_ref=shared.at[z, core, y], dst_ref=shared.at[z, core, y],
            send_sem=asend_sem, recv_sem=arecv_sem.at[off],
            device_id=samp_dev(off, dq), device_id_type=MESH,
        )

    def gather(i, _):
        for dq in (2, 3, 1, 0):
            gather_copy(far_first(i), dq).start()
        return 0

    lax.fori_loop(0, NZ - 1, gather, 0)
    for dq in range(1, NY):
        gather_copy(0, dq).start()

    def forward_copy(off):
        lg = lax.rem(z + NZ - off, NZ)
        return pltpu.make_async_remote_copy(
            src_ref=shared.at[lg, core], dst_ref=shared.at[lg, core],
            send_sem=fsend_sem, recv_sem=frecv_sem.at[off],
            device_id=partner, device_id_type=MESH,
        )

    part = rrecv.at[0, pl.ds(1, NY - 1)]
    pltpu.make_async_copy(part, part, arecv_sem.at[0]).wait()
    forward_copy(0).start()

    def forward(i, _):
        off = near_first(i)
        pltpu.make_async_copy(rrecv.at[0], rrecv.at[0], arecv_sem.at[off]).wait()
        forward_copy(off).start()
        return 0

    lax.fori_loop(1, NZ, forward, 0)

    acc[...] = jnp.zeros_like(acc)
    order = [(dx, dh) for dh in (1, 0) for dx in (2, 1, 3, 0)]
    sections = [lax.rem(x + dx, NX) * NH + lax.rem(yh + dh, NH) for dx, dh in order]

    def second_products(i, _):
        off = near_first(i)
        lg = lax.rem(z + NZ - off, NZ)
        forward_copy(off).wait_recv()
        value = shared[lg].astype(F32).reshape(rhs, group)
        var = (ci * NZ + lg) * group + lax.broadcasted_iota(jnp.int32, (1, group), 1)
        pieces = []
        for c in sections:
            inside = (var >= bounds[0, c]) & (var < bounds[1, c])
            pieces.append((value * jnp.where(inside, 0.0, 1.0)).astype(BF16))
        lhs = jnp.concatenate(pieces, axis=0)
        acc[...] += lax.dot_general(
            lhs, std[lg], (((1,), (1,)), ((), ())), preferred_element_type=F32
        )
        return 0

    lax.fori_loop(0, NZ, second_products, 0)

    def x_copy(j, dx, dh):
        return pltpu.make_async_remote_copy(
            src_ref=xsend.at[j], dst_ref=xrecv.at[j],
            send_sem=xsend_sem.at[j], recv_sem=xrecv_sem.at[j],
            device_id=chrom_dev(dx, 0), device_id_type=MESH,
        )

    for j, (dx, dh) in enumerate(order):
        if dx:
            xsend[j] = acc[j * rhs : (j + 1) * rhs, :].astype(BF16)
            x_copy(j, dx, dh).start()

    def x_sum(first):
        value = acc[(first + NX - 1) * rhs : (first + NX) * rhs, :]
        for j in range(first, first + NX - 1):
            x_copy(j, *order[j]).wait()
            value = value + xrecv[j].astype(F32)
        return value

    ysend[...] = x_sum(0).astype(BF16)
    y_copy = pltpu.make_async_remote_copy(
        src_ref=ysend, dst_ref=yrecv, send_sem=ysend_sem, recv_sem=yrecv_sem,
        device_id=chrom_dev(0, 1), device_id_type=MESH,
    )
    y_copy.start()
    mine = x_sum(NX)
    divisor = (variants - widths_ref[ci]).astype(F32)
    y_copy.wait()
    out_ref[...] = ridge_ref[0] * dir_ref[...] + (mine + yrecv[...].astype(F32)) / divisor

    sent = rrecv.at[pl.ds(1, NZ - 1)]
    rest = rrecv.at[0, pl.ds(1, NY - 1)]
    for sem in (rsend_sem, asend_sem):
        pltpu.make_async_copy(sent, sent, sem).wait()
        pltpu.make_async_copy(rest, rest, sem).wait()
    whole = shared.at[:, 0]
    pltpu.make_async_copy(whole, whole, fsend_sem).wait()


def on_device(genotypes, frequency, widths, ridge_term, direction):
    rows, local_vars = genotypes.shape
    rhs = direction.shape[1]
    group = local_vars // NZ
    half = rhs // NCORE
    piece = half // NY
    sections = NX * NH
    dma, regular = pltpu.SemaphoreType.DMA, pltpu.SemaphoreType.REGULAR
    vmem, smem = pltpu.VMEM, pltpu.SMEM
    out = pl.pallas_call(
        kernel,
        out_shape=jax.ShapeDtypeStruct((rhs, rows), F32),
        in_specs=[
            pl.BlockSpec(memory_space=pl.ANY),
            pl.BlockSpec(memory_space=vmem),
            pl.BlockSpec(memory_space=smem),
            pl.BlockSpec(memory_space=smem),
            pl.BlockSpec(memory_space=vmem),
        ],
        out_specs=pl.BlockSpec(memory_space=vmem),
        scratch_shapes=[
            vmem((NZ, rows, group), jnp.int32),
            vmem((NZ, rows, group), BF16),
            vmem((NZ, rhs, group), F32),
            vmem((NZ, half, group), BF16),
            vmem((NZ, half, group), BF16),
            vmem((NZ, NY, piece, group), BF16),
            vmem((NZ, NY, piece, group), BF16),
            vmem((NZ, NCORE, NY, piece, group), BF16),
            vmem((sections * rhs, rows), F32),
            vmem((sections, rhs, rows), BF16),
            vmem((sections, rhs, rows), BF16),
            vmem((rhs, rows), BF16),
            vmem((rhs, rows), BF16),
            smem((2, sections), jnp.int32),
            dma((NZ,)), dma((NZ,)), dma((NZ,)),
            dma, dma((NZ,)), dma, dma((NZ,)), dma, dma((NZ,)),
            dma((sections,)), dma((sections,)), dma, dma,
        ],
        compiler_params=pltpu.CompilerParams(collective_id=0, has_side_effects=True),
        name="loco",
    )(genotypes, frequency.reshape(1, local_vars), widths, ridge_term, direction.T)
    return out.T[None]


def solution(mesh):
    return jax.shard_map(
        on_device,
        mesh=mesh,
        in_specs=(P("samp", "chrom"), P("chrom"), P(), P(), P("samp", None)),
        out_specs=P("chrom", "samp", None),
        check_vma=False,
    )
```

time: 134 us -> 49.4 us (0.37); the launches traced: 132 us -> 48.9 us
  waiting for transfers between devices: 57.7 us -> 0 us
  Pallas kernels: 0 us -> 46.7 us
  blocking collectives: 28.3 us -> 0 us
  starting transfers between devices: 24.3 us -> 0 us
  matrix products: 8.56 us -> 0 us
  other arithmetic: 5.89 us -> 0 us
  local copies, waits for them, and re-layouts: 5.5 us -> 1.54 us
    all_to_all x3 -> x0, waiting for transfers between devices: 57.7 us -> none  [the longest x2 41.7 us: summed_on_arrival(): lax.all_to_all(blocks, axis, split_axis=0, concat_axis=0, tiled=True)]
    pallas_call x0 -> x1, Pallas kernels: none -> 46.7 us  [on_device(): pl.pallas_call(kernel, out_shape=jax.ShapeDtypeStruct((rhs, rows), F32),...]
    all_to_all x1 -> x0, blocking collectives: 28.3 us -> none  [from_everyone(): return lax.all_to_all(copies, axis, split_axis=0, concat_axis=0, tiled=True)]
    all_to_all x3 -> x0, starting transfers between devices: 24.3 us -> none  [the longest x2 18.9 us: summed_on_arrival(): lax.all_to_all(blocks, axis, split_axis=0, concat_axis=0, tiled=True)]
    dot_general x1 -> x0, matrix products: 5.09 us -> none  [on_device(): partial_value = jnp.dot(columns, spread, preferred_element_type=jnp.float32)]
    reshape x1 -> x0, matrix products: 3.48 us -> none  [cut_along(): return jnp.moveaxis(x.reshape(*before, count, -1, *after), dim, 0)]
    all_to_all x1 -> x0, other arithmetic: 2.51 us -> none  [summed_on_arrival(): lax.all_to_all(blocks, axis, split_axis=0, concat_axis=0, tiled=True)]
    unnamed x8 -> x1, local copies, waits for them, and re-layouts: 3.98 us -> 1.54 us
  transfers between devices with their start and end apart: 3 -> 0, of which waited for: 3 -> 0; matrix products, arithmetic and copies ran while one was open for 1% -> 0% of each run, Pallas kernels for 0% -> 0%
where the time goes in v1:
time: 49.4 us; the launch traced here: 48.9 us
  Pallas kernels  46.7 us (95%)
  local copies, waits for them, and re-layouts  1.54 us (3%)
  between operations  0.66 us (1%)
    pallas_call x1, Pallas kernels, on_device(): pl.pallas_call(kernel, out_shape=jax.ShapeDtypeStruct((rhs, rows), F32),...  46.7 us
    unnamed x1, local copies, waits for them, and re-layouts  1.54 us

profile of v1, /device:TPU:1, one launch (start us, length us, event | category | flops | bytes accessed | tf_op | source)
XLA Modules:
  0.0 48.9 jit_solution(13908561380612128875)
XLA Ops:
  0.7 46.7 %loco.1 = f32[64,384]{1,0:T(8,128)} custom-call(s32[384,3072]{1,0:T(8,128)} %gen_hbm.1, f32[1,3072]{1,0:T(1,128)} %bitcast.7, s32[8]{0:T(128)} %widths_ref.1, f32[1]{0:T(128)S(6)} %copy.7.ridge_ref, f32[64,384]{1,0:T(8,128)} %bitcast.6), custom_call_target="tpu_custom_call" | custom-call | tf_op jit(solution)/shard_map/loco/pallas_call | solution.py:250
  47.4 1.5 %copy.8 = f32[1,384,64]{1,2,0:T(8,128)} copy(f32[1,384,64]{1,2,0:T(8,128)} %bitcast.5) | data formatting | bytes 196608

commit v2 on v1

v2 whole, which is shorter than its diff:
```python
import jax
import jax.numpy as jnp
from jax import lax
from jax.experimental import pallas as pl
from jax.experimental.pallas import tpu as pltpu
from jax.sharding import PartitionSpec as P

MESH = pl.DeviceIdType.MESH
NZ, NY, NCORE = 8, 4, 2
NX, NH = 4, 2
CHUNKS = ((0, 8),)
BF16, F32 = jnp.bfloat16, jnp.float32


def loop(start, stop, body, carry):
    for i in range(start, stop):
        body(i, carry)


def far_first(i):
    half = NZ // 2
    return (half + (i + 1) // 2 if i % 2 else half - i // 2) % NZ


def near_first(i):
    return ((i + 1) // 2 if i % 2 else NZ - i // 2) % NZ


def kernel(
    gen_hbm, freq_hbm, widths_hbm, ridge_hbm, dir_hbm, near_hbm, far_hbm,
    freq_ref, widths_ref, ridge_ref, dir_ref, gbuf, std, own, psend, precv, rsend, rrecv, shared, acc, xsend, xrecv, ysend, near, bounds,
    isem, gsem, psend_sem, precv_sem, rsend_sem, rrecv_sem, asend_sem, arecv_sem, ssend_sem, srecv_sem,
    xsend_sem, xrecv_sem, ysend_sem, yrecv_sem, out_sem, known_sem,
):
    half, rows = dir_ref.shape[1:]
    rhs = NCORE * half
    group = gbuf.shape[2]
    variants = NX * NH * NZ * group
    ci, si = lax.axis_index("chrom"), lax.axis_index("samp")
    z, y, core = si // (NY * NCORE), lax.rem(si // NCORE, NY), lax.rem(si, NCORE)
    x, yh = ci // NH, lax.rem(ci, NH)

    def samp_at(off, q):
        return (ci, (lax.rem(z + off, NZ) * NY + q) * NCORE + core)

    def samp_dev(off, dq):
        return samp_at(off, lax.rem(y + dq, NY))

    partner = (ci, si + 1 - 2 * core)

    def chrom_dev(dx, dh, dc=0):
        other = si + dc * (1 - 2 * core)
        return (lax.rem(x + dx, NX) * NH + lax.rem(yh + dh, NH), other)

    def lane_group(off):
        return lax.rem(z + off, NZ)

    def gcopy(i):
        lanes = pl.ds(pl.multiple_of(lane_group(far_first(i)) * group, 128), group)
        return pltpu.make_async_copy(gen_hbm.at[:, lanes], gbuf.at[i], gsem.at[i])

    def start_gcopy(i, _):
        gcopy(i).start()
        return 0

    small = [
        pltpu.make_async_copy(src, dst, isem.at[k])
        for k, (src, dst) in enumerate(
            (
                (dir_hbm, dir_ref), (freq_hbm, freq_ref),
                (widths_hbm, widths_ref), (ridge_hbm, ridge_ref),
            )
        )
    ]
    for copy in small:
        copy.start()
    loop(0, NZ, start_gcopy, 0)

    barrier = pltpu.get_barrier_semaphore()
    greeted = [samp_dev(off, dq) for off in (2, 6, 1, 7, 0) for dq in (2, 3, 1, 0) if off or dq]
    greeted += [chrom_dev(0, 1)]
    greeted += [chrom_dev(dx, 0, dc) for dx in (2, 1, 3, 0) for dc in range(NCORE) if dx or dc]
    for device in greeted:
        pl.semaphore_signal(barrier, inc=1, device_id=device, device_id_type=MESH)

    for copy in small:
        copy.wait()

    total = jnp.int32(0)
    for c in range(NX * NH):
        bounds[0, c] = total
        total = total + widths_ref[c]
        bounds[1, c] = total

    vector = dir_ref[...].reshape(rhs, rows).astype(BF16)

    def first_products(i, _):
        gcopy(i).wait()
        lg = lane_group(far_first(i))
        freq = freq_ref[:, pl.ds(pl.multiple_of(lg * group, 128), group)]
        doubled = 2.0 * freq
        scale = lax.rsqrt(doubled * (1.0 - freq))
        block = ((gbuf[i].astype(F32) - doubled) * scale).astype(BF16)
        std[lg, core] = block
        value = jnp.dot(vector, block, preferred_element_type=F32)
        own[i] = value
        psend[i] = value.astype(BF16)
        return 0

    loop(0, NZ, first_products, 0)

    pl.semaphore_wait(barrier, len(greeted))
    for off in (2, NZ - 2):
        pl.semaphore_signal(known_sem, inc=1, device_id=samp_dev(off, 0), device_id_type=MESH)

    def pair_copy(i):
        return pltpu.make_async_remote_copy(
            src_ref=psend.at[i, pl.ds(pl.multiple_of((1 - core) * half, half), half)],
            dst_ref=precv.at[i],
            send_sem=psend_sem.at[i], recv_sem=precv_sem.at[i],
            device_id=partner, device_id_type=MESH,
        )

    def pair_start(i, _):
        pair_copy(i).start()
        return 0

    loop(0, NZ, pair_start, 0)

    def scatter_copy(i, off, dq):
        return pltpu.make_async_remote_copy(
            src_ref=rsend.at[i, lax.rem(y + dq, NY)], dst_ref=rrecv.at[off, dq],
            send_sem=rsend_sem, recv_sem=rrecv_sem.at[off],
            device_id=samp_dev(off, dq), device_id_type=MESH,
        )

    def pair_sum(i):
        pair_copy(i).wait()
        mine = pl.multiple_of(core * half, half)
        value = own[i, pl.ds(mine, half), :] + precv[i].astype(F32)
        rsend[i] = value.astype(BF16).reshape(NY, half // NY, group)

    pair_sum(0)
    pl.semaphore_wait(known_sem, 2)

    def scatter(i, _):
        if i:
            pair_sum(i)
        off = far_first(i)
        for dq in (2, 3, 1, 0):
            scatter_copy(i, off, dq).start()
        return 0

    loop(0, NZ - 1, scatter, 0)
    pair_sum(NZ - 1)
    for dq in range(1, NY):
        scatter_copy(NZ - 1, 0, dq).start()

    def std_copy(i):
        lg = lane_group(near_first(i))
        return pltpu.make_async_remote_copy(
            src_ref=std.at[lg, core], dst_ref=std.at[lg, core],
            send_sem=ssend_sem.at[i], recv_sem=srecv_sem.at[i],
            device_id=partner, device_id_type=MESH,
        )

    for i in range(NZ):
        std_copy(i).start()

    block = rsend[NZ - 1, y].astype(F32)
    for off in (0, 1, 7, 2, 6, 3, 5, 4):
        part = rrecv.at[off, pl.ds(1, NY - 1)] if off == 0 else rrecv.at[off]
        pltpu.make_async_copy(part, part, rrecv_sem.at[off]).wait()
        for dq in range(NY):
            if off or dq:
                block = block + rrecv[off, dq].astype(F32)
    shared[z, y] = block.astype(BF16)

    def gather_copy(off, dq):
        return pltpu.make_async_remote_copy(
            src_ref=shared.at[z, y], dst_ref=shared.at[z, y],
            send_sem=asend_sem, recv_sem=arecv_sem.at[off],
            device_id=samp_dev(off, dq), device_id_type=MESH,
        )

    def gather(i, _):
        for dq in (2, 3, 1, 0):
            gather_copy(far_first(i), dq).start()
        return 0

    loop(0, NZ - 1, gather, 0)
    for dq in range(1, NY):
        gather_copy(0, dq).start()

    order = [(dx, dh) for dh in (1, 0) for dx in (2, 1, 3, 0)]
    sections = [lax.rem(x + dx, NX) * NH + lax.rem(yh + dh, NH) for dx, dh in order]

    for i in range(NZ):
        std_copy(i).wait()
    for first, last in CHUNKS:
        left, right = [], []
        for i in range(first, last):
            off = near_first(i)
            lg = lane_group(NZ - off)
            part = rrecv.at[0, pl.ds(1, NY - 1)] if off == 0 else rrecv.at[0]
            pltpu.make_async_copy(part, part, arecv_sem.at[off]).wait()
            value = shared[lg].astype(F32).reshape(half, group)
            var = (ci * NZ + lg) * group + lax.broadcasted_iota(jnp.int32, (1, group), 1)
            pieces = []
            for c in sections:
                inside = (var >= bounds[0, c]) & (var < bounds[1, c])
                pieces.append((value * jnp.where(inside, 0.0, 1.0)).astype(BF16))
            left.append(jnp.concatenate(pieces, axis=0))
            right.append(std[lg].reshape(NCORE * rows, group))
        product = lax.dot_general(
            jnp.concatenate(left, axis=1), jnp.concatenate(right, axis=1),
            (((1,), (1,)), ((), ())), preferred_element_type=F32,
        )
        for dc in range(NCORE):
            part = product[:, dc * rows : (dc + 1) * rows]
            acc[dc] = part if first == 0 else acc[dc] + part

    def x_copy(j, dx, dc):
        return pltpu.make_async_remote_copy(
            src_ref=xsend.at[j, dc], dst_ref=xrecv.at[j, dc],
            send_sem=xsend_sem.at[j, dc], recv_sem=xrecv_sem.at[j, dc],
            device_id=chrom_dev(dx, 0, dc), device_id_type=MESH,
        )

    for j, (dx, dh) in enumerate(order):
        for dc in range(NCORE):
            if dx or dc:
                to = lax.rem(core + dc, NCORE)
                xsend[j, dc] = acc[to, j * half : (j + 1) * half, :].astype(BF16)
                x_copy(j, dx, dc).start()

    def x_sum(first, dc):
        last = first + NX - 1
        value = None if dc else acc[core, last * half : (last + 1) * half, :]
        for j in (range(first, last), (last, *range(first, last)))[dc]:
            x_copy(j, order[j][0], dc).wait()
            part = xrecv[j, dc].astype(F32)
            value = part if value is None else value + part
        return value

    def divisor(c):
        return (variants - widths_ref[c]).astype(F32)

    for dc in (1, 0):
        ysend[lax.rem(core + dc, NCORE)] = (
            x_sum(0, dc) / divisor(ci + 1 - 2 * yh)
        ).astype(BF16)
    y_copy = pltpu.make_async_remote_copy(
        src_ref=ysend, dst_ref=far_hbm, send_sem=ysend_sem, recv_sem=yrecv_sem,
        device_id=chrom_dev(0, 1), device_id_type=MESH,
    )
    y_copy.start()
    for dc in (1, 0):
        rows_of = lax.rem(core + dc, NCORE)
        near[rows_of] = ridge_ref[0, 0] * dir_ref[rows_of] + x_sum(NX, dc) / divisor(ci)
    out_copy = pltpu.make_async_copy(near, near_hbm, out_sem)
    out_copy.start()

    sent = rrecv.at[pl.ds(1, NZ - 1)]
    rest = rrecv.at[0, pl.ds(1, NY - 1)]
    for sem in (rsend_sem, asend_sem):
        pltpu.make_async_copy(sent, sent, sem).wait()
        pltpu.make_async_copy(rest, rest, sem).wait()
    out_copy.wait()
    y_copy.wait()


def on_device(genotypes, frequency, widths, ridge_term, direction):
    rows, local_vars = genotypes.shape
    rhs = direction.shape[1]
    group = local_vars // NZ
    half = rhs // NCORE
    piece = half // NY
    sections = NX * NH
    dma, regular = pltpu.SemaphoreType.DMA, pltpu.SemaphoreType.REGULAR
    vmem, smem = pltpu.VMEM, pltpu.SMEM
    near, far = pl.pallas_call(
        kernel,
        out_shape=[jax.ShapeDtypeStruct((NCORE, half, rows), t) for t in (F32, BF16)],
        in_specs=[pl.BlockSpec(memory_space=pltpu.HBM)] * 5,
        out_specs=[pl.BlockSpec(memory_space=pl.ANY)] * 2,
        scratch_shapes=[
            vmem((1, local_vars), F32),
            smem((sections,), jnp.int32),
            smem((1, 1), F32),
            vmem((NCORE, half, rows), F32),
            vmem((NZ, rows, group), jnp.int32),
            vmem((NZ, NCORE, rows, group), BF16),
            vmem((NZ, rhs, group), F32),
            vmem((NZ, rhs, group), BF16),
            vmem((NZ, half, group), BF16),
            vmem((NZ, NY, piece, group), BF16),
            vmem((NZ, NY, piece, group), BF16),
            vmem((NZ, NY, piece, group), BF16),
            vmem((NCORE, sections * half, rows), F32),
            vmem((sections, NCORE, half, rows), BF16),
            vmem((sections, NCORE, half, rows), BF16),
            vmem((NCORE, half, rows), BF16),
            vmem((NCORE, half, rows), F32),
            smem((2, sections), jnp.int32),
            dma((4,)), dma((NZ,)), dma((NZ,)), dma((NZ,)),
            dma, dma((NZ,)), dma, dma((NZ,)), dma((NZ,)), dma((NZ,)),
            dma((sections, NCORE)), dma((sections, NCORE)), dma, dma, dma, regular,
        ],
        compiler_params=pltpu.CompilerParams(collective_id=0, has_side_effects=True),
        name="loco",
    )(
        genotypes, frequency.reshape(1, local_vars), widths, ridge_term.reshape(1, 1),
        direction.T.reshape(NCORE, half, rows),
    )
    out = (near + far.astype(F32)).reshape(rhs, rows)
    return out.T[None]


def solution(mesh):
    return jax.shard_map(
        on_device,
        mesh=mesh,
        in_specs=(P("samp", "chrom"), P("chrom"), P(), P(), P("samp", None)),
        out_specs=P("chrom", "samp", None),
        check_vma=False,
    )
```

time: 49.4 us -> 44.8 us (0.907)
  Pallas kernels: 46.7 us -> 42.5 us
  other arithmetic: 0 us -> 1.55 us
  local copies, waits for them, and re-layouts: 1.54 us -> 0 us
    pallas_call x1, Pallas kernels: 46.7 us -> 42.5 us  [on_device(): pl.pallas_call(kernel, out_shape=[jax.ShapeDtypeStruct((NCORE, half, rows...]
    add x0 -> x1, other arithmetic: none -> 1.55 us  [on_device(): out = (near + far.astype(F32)).reshape(rhs, rows)]
    unnamed x1 -> x0, local copies, waits for them, and re-layouts: 1.54 us -> none
where the time goes in v2:
time: 44.8 us; the launch traced here: 44.7 us
  Pallas kernels  42.5 us (95%)
  other arithmetic  1.55 us (3%)
  between operations  0.66 us (1%)
    pallas_call x1, Pallas kernels, on_device(): pl.pallas_call(kernel, out_shape=[jax.ShapeDtypeStruct((NCORE, half, rows...  42.5 us
    add x1, other arithmetic, on_device(): out = (near + far.astype(F32)).reshape(rhs, rows)  1.55 us

profile of v2, /device:TPU:1, one launch (start us, length us, event | category | flops | bytes accessed | tf_op | source)
XLA Modules:
  0.0 44.7 jit_solution(1713451854466843137)
XLA Ops:
  0.7 42.5 %loco.1 = (f32[2,32,384]{2,1,0:T(8,128)}, bf16[2,32,384]{2,1,0:T(8,128)(2,1)}) custom-call(s32[384,3072]{1,0:T(8,128)} %gen_hbm.1, f32[1,3072]{1,0:T(1,128)} %bitcast.12, s32[8]{0:T(128)} %widths_hbm.1, f32[1,1]{1,0:T(1,128)} %bitcast.10.ridge_hbm, f32[2,32,384]{2,1,0:T(8,128)} %bitcast.11), custom_call_target="tpu_custom_call" | custom-call | tf_op jit(solution)/shard_map/loco/pallas_call | solution.py:282
  43.1 1.5 %convert_add_fusion = f32[2,32,384]{2,1,0:T(8,128)} fusion(f32[2,32,384]{2,1,0:T(8,128)} %get-tuple-element.7, bf16[2,32,384]{2,1,0:T(8,128)(2,1)} %get-tuple-element.8), kind=kLoop, calls=%fused_computation | loop fusion | flops 49152 | bytes 245760 | tf_op jit(solution)/shard_map/add | solution.py:316

commit v3 on v2

--- a/solution.py
+++ b/solution.py
@@ -246,15 +246,19 @@
     def divisor(c):
         return (variants - widths_ref[c]).astype(F32)
 
-    for dc in (1, 0):
+    def y_copy(dc):
+        rows_of = lax.rem(core + dc, NCORE)
+        return pltpu.make_async_remote_copy(
+            src_ref=ysend.at[rows_of], dst_ref=far_hbm.at[rows_of],
+            send_sem=ysend_sem.at[dc], recv_sem=yrecv_sem.at[dc],
+            device_id=chrom_dev(0, 1), device_id_type=MESH,
+        )
+
+    for dc in (0, 1):
         ysend[lax.rem(core + dc, NCORE)] = (
             x_sum(0, dc) / divisor(ci + 1 - 2 * yh)
         ).astype(BF16)
-    y_copy = pltpu.make_async_remote_copy(
-        src_ref=ysend, dst_ref=far_hbm, send_sem=ysend_sem, recv_sem=yrecv_sem,
-        device_id=chrom_dev(0, 1), device_id_type=MESH,
-    )
-    y_copy.start()
+        y_copy(dc).start()
     for dc in (1, 0):
         rows_of = lax.rem(core + dc, NCORE)
         near[rows_of] = ridge_ref[0, 0] * dir_ref[rows_of] + x_sum(NX, dc) / divisor(ci)
@@ -267,7 +271,8 @@
         pltpu.make_async_copy(sent, sent, sem).wait()
         pltpu.make_async_copy(rest, rest, sem).wait()
     out_copy.wait()
-    y_copy.wait()
+    for dc in range(NCORE):
+        y_copy(dc).wait()
 
 
 def on_device(genotypes, frequency, widths, ridge_term, direction):
@@ -305,7 +310,8 @@
             smem((2, sections), jnp.int32),
             dma((4,)), dma((NZ,)), dma((NZ,)), dma((NZ,)),
             dma, dma((NZ,)), dma, dma((NZ,)), dma((NZ,)), dma((NZ,)),
-            dma((sections, NCORE)), dma((sections, NCORE)), dma, dma, dma, regular,
+            dma((sections, NCORE)), dma((sections, NCORE)),
+            dma((NCORE,)), dma((NCORE,)), dma, regular,
         ],
         compiler_params=pltpu.CompilerParams(collective_id=0, has_side_effects=True),
         name="loco",

time: 44.8 us -> 44.2 us (0.987)
  Pallas kernels: 42.5 us -> 41.8 us
    pallas_call x1, Pallas kernels: 42.5 us -> 41.8 us  [on_device(): pl.pallas_call(kernel, out_shape=[jax.ShapeDtypeStruct((NCORE, half, rows...]
where the time goes in v3:
time: 44.2 us; the launch traced here: 44 us
  Pallas kernels  41.8 us (95%)
  other arithmetic  1.55 us (4%)
  between operations  0.66 us (1%)
    pallas_call x1, Pallas kernels, on_device(): pl.pallas_call(kernel, out_shape=[jax.ShapeDtypeStruct((NCORE, half, rows...  41.8 us
    add x1, other arithmetic, on_device(): out = (near + far.astype(F32)).reshape(rhs, rows)  1.55 us

profile of v3, /device:TPU:1, one launch (start us, length us, event | category | flops | bytes accessed | tf_op | source)
XLA Modules:
  0.0 44.0 jit_solution(1117829003438307996)
XLA Ops:
  0.7 41.8 %loco.1 = (f32[2,32,384]{2,1,0:T(8,128)}, bf16[2,32,384]{2,1,0:T(8,128)(2,1)}) custom-call(s32[384,3072]{1,0:T(8,128)} %gen_hbm.1, f32[1,3072]{1,0:T(1,128)} %bitcast.12, s32[8]{0:T(128)} %widths_hbm.1, f32[1,1]{1,0:T(1,128)} %bitcast.10.ridge_hbm, f32[2,32,384]{2,1,0:T(8,128)} %bitcast.11), custom_call_target="tpu_custom_call" | custom-call | tf_op jit(solution)/shard_map/loco/pallas_call | solution.py:287
  42.5 1.5 %convert_add_fusion = f32[2,32,384]{2,1,0:T(8,128)} fusion(f32[2,32,384]{2,1,0:T(8,128)} %get-tuple-element.7, bf16[2,32,384]{2,1,0:T(8,128)(2,1)} %get-tuple-element.8), kind=kLoop, calls=%fused_computation | loop fusion | flops 49152 | bytes 245760 | tf_op jit(solution)/shard_map/add | solution.py:322

commit v4 on v3

--- a/solution.py
+++ b/solution.py
@@ -18,8 +18,7 @@
 
 
 def far_first(i):
-    half = NZ // 2
-    return (half + (i + 1) // 2 if i % 2 else half - i // 2) % NZ
+    return (4, 3, 5, 2, 6, 1, 7, 0)[i]
 
 
 def near_first(i):

time: 44.2 us -> 44.4 us (level)
  no operation moved by 1% of the time
where the time goes in v4:
time: 44.4 us; the launch traced here: 44.2 us
  Pallas kernels  42 us (95%)
  other arithmetic  1.55 us (3%)
  between operations  0.66 us (1%)
    pallas_call x1, Pallas kernels, on_device(): pl.pallas_call(kernel, out_shape=[jax.ShapeDtypeStruct((NCORE, half, rows...  42 us
    add x1, other arithmetic, on_device(): out = (near + far.astype(F32)).reshape(rhs, rows)  1.55 us

profile of v4, /device:TPU:1, one launch (start us, length us, event | category | flops | bytes accessed | tf_op | source)
XLA Modules:
  0.0 44.2 jit_solution(3689595878666965511)
XLA Ops:
  0.7 42.0 %loco.1 = (f32[2,32,384]{2,1,0:T(8,128)}, bf16[2,32,384]{2,1,0:T(8,128)(2,1)}) custom-call(s32[384,3072]{1,0:T(8,128)} %gen_hbm.1, f32[1,3072]{1,0:T(1,128)} %bitcast.12, s32[8]{0:T(128)} %widths_hbm.1, f32[1,1]{1,0:T(1,128)} %bitcast.10.ridge_hbm, f32[2,32,384]{2,1,0:T(8,128)} %bitcast.11), custom_call_target="tpu_custom_call" | custom-call | tf_op jit(solution)/shard_map/loco/pallas_call | solution.py:286
  42.7 1.5 %convert_add_fusion = f32[2,32,384]{2,1,0:T(8,128)} fusion(f32[2,32,384]{2,1,0:T(8,128)} %get-tuple-element.7, bf16[2,32,384]{2,1,0:T(8,128)(2,1)} %get-tuple-element.8), kind=kLoop, calls=%fused_computation | loop fusion | flops 49152 | bytes 245760 | tf_op jit(solution)/shard_map/add | solution.py:321
